TPU v7x, 32 devices: a whole 2x2x4 slice. The times are simulated.
32 devices in a mesh: groups: 2 (over y), vocab: 4 (over z), edit: 2 (over x), tok: 2 (over core).
Axes of the slice: x: 2, y: 2, z: 4, core: 2. Of those that a mesh axis runs over, the one named last changes fastest.
Arguments:
- token_ids: int32 [256], P(('groups', 'tok')), parts along dimension 0, may hold values from 0 to 4095
- valid_mask: int32 [256], P(('groups', 'tok')), parts along dimension 0, may hold values 0 or 1
- key_index: int32 [4], P('groups'), parts along dimension 0, may hold values from 0 to 3
- hidden_act: bfloat16 [256, 14336], P(('groups', 'tok'), 'vocab'), parts along dimension 0, may hold values from -6 to 6
- key_table: bfloat16 [4, 14336], P(None, 'vocab'), may hold values from -0.046875 to 0.046875
- base_out: bfloat16 [256, 4096], P(('groups', 'tok'), 'vocab'), parts along dimension 0, may hold values from -50 to 50
- value_vecs: bfloat16 [4, 4096], P(('groups', 'edit'), 'vocab'), parts along dimension 0, may hold values from -6 to 6
- norm_gain: float32 [4096], replicated, may hold values from 0.5 to 1.5
- head: bfloat16 [4096, 4096], P(('vocab', 'edit')), may hold values from -46 to 46
Outputs:
- grad_value: float32 [4, 4096], P(('groups', 'edit'), 'vocab'), parts along dimension 0
- token_kl: float32 [4, 128], P(('groups', 'edit'), 'tok'), parts along dimension 0
- target_logprob: float32 [4, 128], P(('groups', 'edit'), 'tok'), parts along dimension 0
There are 2 independent parts, one for each index of `groups`. A program takes and returns all parts, laid end to end along the dimension named above; an argument that names none is the same for every part. Nothing has to cross between parts.
All inputs are finite; a program needn't handle non-finite values. No bound on the sum of `valid_mask` on one device may be relied on, other than what follows from the above.
Results may differ from a plain program's by a relative error of at most 0.0061.
Values may be sent and summed in bfloat16 or wider, within the bound.
A program may use at most 64 MiB of HBM per device.

v0:
```python
import jax
import jax.numpy as jnp
from jax import lax
from jax.sharding import PartitionSpec as P

NORM_EPS = 1e-05


def rms_scale(hidden_rows):
    return lax.rsqrt(jnp.mean(hidden_rows * hidden_rows, axis=-1, keepdims=True) + NORM_EPS)


def per_device(
    token_ids, valid_mask, key_index, hidden_act, key_table, base_out, value_vecs, norm_gain, head
):
    vocab_rows = head.shape[0]
    edit_rows = value_vecs.shape[0]
    piece_width = value_vecs.shape[1]
    key_slots = jnp.arange(key_table.shape[0], dtype=jnp.int32)
    select = (key_index[:, None] == key_slots[None, :]).astype(jnp.bfloat16)
    edit_keys = jnp.dot(select, key_table, preferred_element_type=jnp.float32).astype(jnp.bfloat16)
    coeff_part = lax.dot_general(
        edit_keys, hidden_act, (((1,), (1,)), ((), ())), preferred_element_type=jnp.float32
    )
    coeff = lax.psum(coeff_part, "vocab")
    base_rows, local_values = (
        lax.all_gather(base_out, "vocab", axis=1, tiled=True),
        lax.all_gather(value_vecs, "vocab", axis=1, tiled=True),
    )
    values = lax.all_gather(local_values, "edit", axis=0, tiled=True)
    base32 = base_rows.astype(jnp.float32)
    base_norm = (norm_gain * base32 * rms_scale(base32)).astype(jnp.bfloat16)
    base_logits = lax.dot_general(
        base_norm, head, (((1,), (1,)), ((), ())), preferred_element_type=jnp.float32
    )
    edited = base32[None, :, :] + coeff[:, :, None] * values.astype(jnp.float32)[:, None, :]
    row_scale = rms_scale(edited)
    normed = (norm_gain * edited * row_scale).astype(jnp.bfloat16)
    logits = jnp.einsum("etd,vd->etv", normed, head, preferred_element_type=jnp.float32)
    vocab_start = lax.axis_index(("vocab", "edit")) * vocab_rows
    vocab_ids = vocab_start + jnp.arange(vocab_rows, dtype=jnp.int32)
    onehot = (token_ids[:, None] == vocab_ids[None, :]).astype(jnp.float32)
    peak_base = jnp.max(base_logits, axis=-1)
    peak_edit = jnp.max(logits, axis=-1)
    peak_base, peak_edit = lax.pmax((peak_base, peak_edit), ("vocab", "edit"))
    base_exp = jnp.exp(base_logits - peak_base[:, None])
    base_total = jnp.sum(base_exp, axis=-1)
    edit_total = jnp.sum(jnp.exp(logits - peak_edit[:, :, None]), axis=-1)
    cross_sum = jnp.sum(base_exp[None, :, :] * (base_logits[None, :, :] - logits), axis=-1)
    target = jnp.sum(onehot[None, :, :] * logits, axis=-1)
    base_total, edit_total, cross_sum, target = lax.psum(
        (base_total, edit_total, cross_sum, target), ("vocab", "edit")
    )
    base_lse = peak_base + jnp.log(base_total)
    edit_lse = peak_edit + jnp.log(edit_total)
    valid = valid_mask.astype(jnp.float32)
    token_kl = valid[None, :] * (cross_sum / base_total[None, :] - base_lse[None, :] + edit_lse)
    target_logprob = target - edit_lse
    base_prob = jnp.exp(base_logits - base_lse[:, None])
    edit_prob = jnp.exp(logits - edit_lse[:, :, None])
    logit_grad = (valid[None, :, None] * (edit_prob - base_prob[None, :, :])).astype(jnp.bfloat16)
    back_rows = jnp.einsum("etv,vd->etd", logit_grad, head, preferred_element_type=jnp.float32)
    grad_y = norm_gain * back_rows
    grad_o = row_scale * grad_y - edited * row_scale**3 * jnp.mean(
        grad_y * edited, axis=-1, keepdims=True
    )
    grad_part = jnp.sum(coeff[:, :, None] * grad_o, axis=1)
    edit_start = lax.axis_index("edit") * edit_rows
    grad_total = lax.psum(grad_part, ("vocab", "edit", "tok"))
    grad_mine = lax.dynamic_slice_in_dim(grad_total, edit_start, edit_rows, 0)
    grad_piece = lax.dynamic_slice_in_dim(
        grad_mine, lax.axis_index("vocab") * piece_width, piece_width, 1
    )
    kl_mine = lax.dynamic_slice_in_dim(token_kl, edit_start, edit_rows, 0)
    target_mine = lax.dynamic_slice_in_dim(target_logprob, edit_start, edit_rows, 0)
    return (grad_piece, kl_mine, target_mine)


def solution(mesh):
    placed = (
        P(("groups", "tok")),
        P(("groups", "tok")),
        P("groups"),
        P(("groups", "tok"), "vocab"),
        P(None, "vocab"),
        P(("groups", "tok"), "vocab"),
        P(("groups", "edit"), "vocab"),
        P(),
        P(("vocab", "edit"), None),
    )
    return jax.shard_map(
        per_device,
        mesh=mesh,
        in_specs=placed,
        out_specs=(
            P(("groups", "edit"), "vocab"),
            P(("groups", "edit"), "tok"),
            P(("groups", "edit"), "tok"),
        ),
        check_vma=False,
    )
```

profile of v0, /device:TPU:0, one launch (start us, length us, event | category | flops | bytes accessed | tf_op | source)
XLA Modules:
  0.0 156.0 jit_solution(18408327459742363050)
XLA Ops:
  0.6 0.0 copy-start
  0.7 0.7 convert_element_type.32
  1.4 0.3 copy-done
  1.7 1.1 fusion.3
  2.8 13.4 %psum.42 = f32[2,64]{1,0:T(2,128)S(1)} all-reduce(f32[2,64]{1,0:T(2,128)S(1)} %fusion.3), channel_id=1, replica_groups=mesh['groups'=2,'vocab'=4,'edit'=2,'tok'=2] {'vocab'}, use_global_device_ids=true, to_apply=%region_0.0 | all-reduce | flops 128 | bytes 1024 | tf_op jit(solution)/shard_map/psum | solution.py:25
  16.3 13.3 %all_gather.10 = bf16[1,4096]{1,0:T(2,128)(2,1)S(1)} all-gather(bf16[1,1024]{1,0:T(2,128)(2,1)} %param.15), channel_id=1, replica_groups=mesh['groups'=2,'vocab'=4,'edit'=2,'tok'=2] {'vocab'}, dimensions={1}, use_global_device_ids=true | all-gather | bytes 10240 | tf_op jit(solution)/shard_map/all_gather | solution.py:28
  29.5 4.4 %all-gather = bf16[2,1,4096]{2,1,0:T(2,128)(2,1)S(1)} all-gather(bf16[1,1,4096]{2,1,0:T(2,128)(2,1)S(1)} %bitcast.20), channel_id=1, replica_groups=mesh['groups'=2,'vocab'=4,'edit'=2,'tok'=2] {'edit'}, dimensions={0}, use_global_device_ids=true | all-gather | bytes 24576 | tf_op jit(solution)/shard_map/all_gather | solution.py:30
  34.0 0.7 compare_convert_fusion
  34.7 15.0 %all_gather.9 = bf16[64,4096]{1,0:T(8,128)(2,1)S(1)} all-gather(bf16[64,1024]{1,0:T(8,128)(2,1)} %param.14), channel_id=1, replica_groups=mesh['groups'=2,'vocab'=4,'edit'=2,'tok'=2] {'vocab'}, dimensions={1}, use_global_device_ids=true | all-gather | bytes 655360 | tf_op jit(solution)/shard_map/all_gather | solution.py:27
  49.7 0.2 multiply_reduce_fusion.3
  49.9 0.0 copy-start.1
  49.9 3.9 %fusion.24 = (f32[64]{0:T(128)S(1)}, f32[64,512]{1,0:T(8,128)S(1)}) fusion(bf16[512,4096]{1,0:T(8,128)(2,1)} %param.17, f32[64]{0:T(128)S(1)} %add_rsqrt_fusion.1, f32[4096]{0:T(1024)} %param.16, bf16[64,4096]{1,0:T(8,128)(2,1)S(1)} %all_gather.9), kind=kOutput, calls=%fused_computation.48 | convolution fusion | flops 269516736 | bytes 4866560 | tf_op jit(solution)/shard_map/dot_general | solution.py:33
  53.8 0.0 copy-start.2
  53.8 0.1 convert_element_type.30
  53.9 0.4 multiply_reduce_fusion.2
  54.3 0.0 copy-done.1
  54.3 0.2 copy-done.2
  54.5 1.6 %fusion.25 = (f32[2,64]{1,0:T(2,128)S(1)}, f32[2,64,512]{2,1,0:T(8,128)S(1)}) fusion(bf16[512,4096]{1,0:T(8,128)(2,1)S(1)} %copy-done.1, f32[4096]{0:T(1024)S(1)} %copy-done.2, f32[2,64]{1,0:T(2,128)S(1)} %get-tuple-element.17, f32[2,4096]{1,0:T(2,128)S(1)} %bitcast.17, f32[64,4096]{1,0:T(8,128)S(1)} %convert_element_type.30, f32[2,64]{1,0:T(2,128)S(1)} %psum.42), kind=kOutput, calls=%fused_computation.49 | convolution fusion | flops 539557760 | bytes 5555712 | tf_op jit(solution)/shard_map/etd,vd->etv/dot_general | solution.py:39
  56.1 18.6 %all-reduce.1 = (f32[64]{0:T(128)S(1)}, f32[2,64]{1,0:T(2,128)S(1)}) all-reduce(f32[64]{0:T(128)S(1)} %get-tuple-element.18, f32[2,64]{1,0:T(2,128)S(1)} %get-tuple-element.20), channel_id=1, replica_groups=mesh['groups'=2,'vocab'=4,'edit'=2,'tok'=2] {'vocab','edit'}, use_global_device_ids=true, to_apply=%region_8.0 | all-reduce | flops 192 | bytes 1536 | tf_op jit(solution)/shard_map/pmax | solution.py:45
  74.7 0.2 fusion.23
  74.9 0.2 multiply_reduce_fusion.4
  75.1 17.7 %all-reduce = (f32[64]{0:T(128)S(1)}, f32[2,64]{1,0:T(2,128)S(1)}, f32[2,64]{1,0:T(2,128)S(1)}, f32[2,64]{1,0:T(2,128)S(1)}) all-reduce(f32[64]{0:T(128)S(1)} %get-tuple-element.14, f32[2,64]{1,0:T(2,128)S(1)} %get-tuple-element.5, ...), channel_id=1, replica_groups=mesh['groups'=2,'vocab'=4,'edit'=2,'tok'=2] {'vocab','edit'}, use_global_device_ids=true, to_apply=%region_10.0 | all-reduce | flops 448 | bytes 3584 | tf_op jit(solution)/shard_map/psum | solution.py:51
  92.8 0.1 subtract_exponential_fusion
  92.9 0.5 constant_dynamic-slice_fusion
  93.4 3.4 %multiply_reduce_fusion.1 = (f32[2,64]{1,0:T(2,128)S(1)}, f32[2,64,4096]{2,1,0:T(8,128)S(1)}) fusion(f32[2,4096]{1,0:T(2,128)S(1)} %bitcast.18, f32[64,4096]{1,0:T(8,128)S(1)} %convert_element_type.30, f32[2,64]{1,0:T(2,128)S(1)} %psum.42, bf16[512,4096]{1,0:T(8,128)(2,1)} %param.17, f32[2,64,512]{2,1,0:T(8,128)S(1)} %get-tuple-element.21, ...), kind=kOutput, calls=%fused_computation.6 | convolution fusion | flops 539754368 | bytes 7784192 | tf_op jit(solution)/shard_map/etv,vd->etd/dot_general | solution.py:62
  96.9 0.8 multiply_reduce_fusion
  97.7 57.6 %psum.45 = f32[2,4096]{1,0:T(2,128)S(1)} all-reduce(f32[2,4096]{1,0:T(2,128)S(1)} %multiply_reduce_fusion), channel_id=1, replica_groups=mesh['groups'=2,'vocab'=4,'edit'=2,'tok'=2] {'vocab','edit','tok'}, use_global_device_ids=true, to_apply=%region_13.0 | all-reduce | flops 8192 | bytes 65536 | tf_op jit(solution)/shard_map/psum | solution.py:69
  155.3 0.7 dynamic_slice.10
  (8 shorter events, 0.1 us)
Async XLA Ops:
  0.6 1.0 copy-start
  49.9 4.4 %copy-start.1 = (bf16[512,4096]{1,0:T(8,128)(2,1)S(1)}, bf16[512,4096]{1,0:T(8,128)(2,1)}, u32[]{:S(2)}) copy-start(bf16[512,4096]{1,0:T(8,128)(2,1)} %param.17) | copy-start | bytes 12582916
  53.8 0.7 copy-start.2
where the time goes:
time: 156 us
  blocking collectives  140 us (90%)
  matrix products  10 us (6%)
  other arithmetic  3.51 us (2%)
  local copies, waits for them, and re-layouts  1.73 us (1%)
    psum x1, blocking collectives, per_device(): grad_total = lax.psum(grad_part, ('vocab', 'edit', 'tok'))  57.6 us
    pmax x1, blocking collectives, per_device(): peak_base, peak_edit = lax.pmax((peak_base, peak_edit), ('vocab', 'edit'))  18.6 us
    psum x1, blocking collectives, per_device(): lax.psum((base_total, edit_total, cross_sum, target), ('vocab', 'edit'))  17.7 us
    all_gather x1, blocking collectives, per_device(): lax.all_gather(base_out, 'vocab', axis=1, tiled=True)  15 us
    psum x1, blocking collectives, per_device(): coeff = lax.psum(coeff_part, 'vocab')  13.4 us
    all_gather x1, blocking collectives, per_device(): lax.all_gather(value_vecs, 'vocab', axis=1, tiled=True)  13.3 us
    all_gather x1, blocking collectives, per_device(): values = lax.all_gather(local_values, 'edit', axis=0, tiled=True)  4.4 us
    dot_general x1, matrix products, per_device(): lax.dot_general(base_norm, head, (((1,), (1,)), ((), ())), preferred_elem...  3.87 us

commit v1 on v0

--- a/solution.py
+++ b/solution.py
@@ -1,6 +1,10 @@
+import functools
+
 import jax
 import jax.numpy as jnp
 from jax import lax
+from jax.experimental import pallas as pl
+from jax.experimental.pallas import tpu as pltpu
 from jax.sharding import PartitionSpec as P
 
 NORM_EPS = 1e-05
@@ -76,6 +80,352 @@
     return (grad_piece, kl_mine, target_mine)
 
 
+MESH = pl.DeviceIdType.MESH
+
+
+def split_rows(row, where_mask):
+    hi = row.astype(jnp.bfloat16).astype(jnp.float32)
+    rest = row - hi
+    mid = rest.astype(jnp.bfloat16).astype(jnp.float32)
+    low = rest - mid
+    at = lax.broadcasted_iota(jnp.int32, (8, row.shape[1]), 0)
+    rows = jnp.where(at == 0, hi, jnp.where(at == 1, mid, jnp.where(at == 2, low, 0.0)))
+    return rows if where_mask is None else jnp.where(where_mask, rows, 0.0)
+
+
+def fused(
+    nv,
+    key_ref,
+    ids_ref,
+    mask_ref,
+    act_hbm,
+    table_ref,
+    base_hbm,
+    val_ref,
+    gain_ref,
+    head_hbm,
+    grad_ref,
+    kl_ref,
+    tl_ref,
+    act,
+    head,
+    rows_all,
+    vals,
+    myval,
+    cpart,
+    call,
+    normed,
+    stat,
+    stats,
+    wmine,
+    wother,
+    smine,
+    sother,
+    gpart,
+    gall,
+    local_sem,
+    head_sem,
+    zs,
+    zr,
+    xs,
+    xr,
+    vs,
+    vr,
+    cs,
+    cr,
+    ss,
+    sr,
+    gs,
+    gr,
+    ts,
+    tr,
+):
+    f32, bf16 = jnp.float32, jnp.bfloat16
+    z = lax.axis_index("vocab")
+    x = lax.axis_index("edit")
+    c = lax.axis_index("tok")
+    q = z * 2 + x
+    nq = nv * 2
+    tk, width = base_hbm.shape
+    half = tk // 2
+    dim = gain_ref.shape[1]
+    vrows = head_hbm.shape[0]
+    hv = vrows // 4
+
+    barrier = pltpu.get_barrier_semaphore()
+    peers = []
+    for k in range(1, nq):
+        p = lax.rem(q + k, nq)
+        peers.append({"vocab": p // 2, "edit": lax.rem(p, 2)})
+    buddy = {"tok": 1 - c}
+    for p in peers:
+        pl.semaphore_signal(barrier, inc=1, device_id=p, device_id_type=MESH)
+    pl.semaphore_signal(barrier, inc=1, device_id=buddy, device_id_type=MESH)
+
+    base_in = pltpu.make_async_copy(base_hbm, rows_all.at[z], local_sem.at[0])
+    base_in.start()
+    act_in = pltpu.make_async_copy(act_hbm, act, local_sem.at[1])
+    act_in.start()
+    head_in = [
+        pltpu.make_async_copy(
+            head_hbm.at[pl.ds(i * hv, hv)], head.at[pl.ds(i * hv, hv)], head_sem.at[i]
+        )
+        for i in range(4)
+    ]
+    for d in head_in:
+        d.start()
+    myval[...] = val_ref[...].astype(f32)
+    vals[x, z] = myval[...]
+    base_in.wait()
+    pl.semaphore_wait(barrier, nq)
+
+    mine = pl.ds(pl.multiple_of(x * half, half), half)
+
+    def send(src, dst, ssem, rsem, dev):
+        d = pltpu.make_async_remote_copy(
+            src_ref=src, dst_ref=dst, send_sem=ssem, recv_sem=rsem, device_id=dev, device_id_type=MESH
+        )
+        d.start()
+        return d
+
+    order = [1, nv - 1] + [k for k in range(2, nv - 1)]
+    zcopies = {}
+    for k in order:
+        zcopies[k] = send(
+            rows_all.at[z, mine], rows_all.at[z, mine], zs.at[k], zr.at[k], {"vocab": lax.rem(z + k, nv)}
+        )
+    vcopies = [
+        send(myval, vals.at[x, z], vs.at[k], vr.at[k], peers[k]) for k in range(nq - 1)
+    ]
+
+    act_in.wait()
+    every = lax.dot_general(
+        table_ref[...], act[...], (((1,), (1,)), ((), ())), preferred_element_type=f32
+    )
+    picked = []
+    for e in range(2):
+        one = jnp.zeros((1, tk), f32)
+        for k in range(every.shape[0]):
+            one = one + jnp.where(key_ref[e] == k, every[k : k + 1, :], 0.0)
+        picked.append(one)
+    for e in range(2):
+        cpart[e] = picked[e]
+    call[z] = cpart[...]
+    ccopies = [
+        send(cpart, call.at[z], cs.at[k], cr.at[k], {"vocab": lax.rem(z + k, nv)})
+        for k in range(1, nv)
+    ]
+
+    sub = lax.broadcasted_iota(jnp.int32, (tk, 2 * tk), 0)
+    lane = lax.broadcasted_iota(jnp.int32, (tk, 2 * tk), 1)
+    first = lane < tk
+    diag = jnp.where(first, lane, lane - tk) == sub
+    eye = lax.broadcasted_iota(jnp.int32, (tk, tk), 0) == lax.broadcasted_iota(
+        jnp.int32, (tk, tk), 1
+    )
+
+    def to_col(row):
+        return jnp.sum(jnp.where(eye, row, 0.0), axis=1, keepdims=True)
+
+    def to_row(col0, col1):
+        return jnp.sum(
+            jnp.where(diag, jnp.where(first, col0, col1), 0.0), axis=0, keepdims=True
+        )
+
+    ids_col = to_col(ids_ref[...].astype(f32))
+    ids_row = to_row(ids_col, ids_col)
+    valid_col = to_col(mask_ref[...].astype(f32))
+    valid = to_row(valid_col, valid_col)
+
+    xcopies = []
+    for k in order:
+        zcopies[k].wait_recv()
+        s = lax.rem(z - k + nv, nv)
+        xcopies.append(
+            send(
+                rows_all.at[s, mine], rows_all.at[s, mine], xs.at[k], xr.at[k], {"edit": 1 - x}
+            )
+        )
+    for d in ccopies:
+        d.wait_recv()
+    for d in vcopies:
+        d.wait_recv()
+    coeff = []
+    for e in range(2):
+        total = call[0, e]
+        for s in range(1, nv):
+            total = total + call[s, e]
+        coeff.append(to_col(total))
+    for d in xcopies:
+        d.wait_recv()
+
+    sq = [jnp.zeros((tk, 1), f32) for _ in range(3)]
+    for s in range(nv):
+        b = rows_all[s].astype(f32)
+        sq[0] = sq[0] + jnp.sum(b * b, axis=1, keepdims=True)
+        for e in range(2):
+            ed = b + coeff[e] * vals[e, s]
+            sq[1 + e] = sq[1 + e] + jnp.sum(ed * ed, axis=1, keepdims=True)
+    scale = [lax.rsqrt(t / dim + NORM_EPS) for t in sq]
+    for s in range(nv):
+        cols = pl.ds(s * width, width)
+        b = rows_all[s].astype(f32)
+        gain = gain_ref[:, cols]
+        plain = (gain * b * scale[0]).astype(bf16)
+        normed[0:tk, cols] = plain
+        normed[tk : 2 * tk, cols] = plain
+        for e in range(2):
+            ed = b + coeff[e] * vals[e, s]
+            normed[(2 + e) * tk : (3 + e) * tk, cols] = (gain * ed * scale[1 + e]).astype(bf16)
+    for d in head_in:
+        d.wait()
+    logit = lax.dot_general(
+        head[...], normed[...], (((1,), (1,)), ((), ())), preferred_element_type=f32
+    )
+    lb, le = logit[:, : 2 * tk], logit[:, 2 * tk :]
+    vid = (q * vrows + lax.broadcasted_iota(jnp.int32, lb.shape, 0)).astype(f32)
+    mb = jnp.max(lb, axis=0, keepdims=True)
+    me = jnp.max(le, axis=0, keepdims=True)
+    eb = jnp.exp(lb - mb)
+    ee = jnp.exp(le - me)
+    stat[0:1] = mb
+    stat[1:2] = me
+    stat[2:3] = jnp.sum(eb, axis=0, keepdims=True)
+    stat[3:4] = jnp.sum(ee, axis=0, keepdims=True)
+    stat[4:5] = jnp.sum(eb * (lb - le), axis=0, keepdims=True)
+    stat[5:6] = jnp.sum(eb * le, axis=0, keepdims=True)
+    stat[6:7] = jnp.sum(ee * le, axis=0, keepdims=True)
+    stat[7:8] = jnp.sum(jnp.where(vid == ids_row, le, 0.0), axis=0, keepdims=True)
+    stats[q] = stat[...]
+    scopies = [send(stat, stats.at[q], ss.at[k], sr.at[k], peers[k]) for k in range(nq - 1)]
+    cr_row = to_row(coeff[0] * scale[1], coeff[1] * scale[2])
+    crr_row = to_row(coeff[0] * scale[1] * scale[1], coeff[1] * scale[2] * scale[2])
+    lanes8 = lax.broadcasted_iota(jnp.int32, (8, 2 * tk), 1)
+    lhs = jnp.concatenate(
+        [split_rows(cr_row, lanes8 < tk), split_rows(cr_row, lanes8 >= tk)], axis=0
+    ).astype(bf16)
+    for d in scopies:
+        d.wait_recv()
+
+    pb, pe = stats[0, 0:1], stats[0, 1:2]
+    for p in range(1, nq):
+        pb = jnp.maximum(pb, stats[p, 0:1])
+        pe = jnp.maximum(pe, stats[p, 1:2])
+    sums = [jnp.zeros((1, 2 * tk), f32) for _ in range(6)]
+    for p in range(nq):
+        fb = jnp.exp(stats[p, 0:1] - pb)
+        fe = jnp.exp(stats[p, 1:2] - pe)
+        for j, f in enumerate((fb, fe, fb, fb, fe, None)):
+            got = stats[p, 2 + j : 3 + j]
+            sums[j] = sums[j] + (got if f is None else f * got)
+    tb, te, cross, meanb, meane, target = sums
+    lse_b = pb + jnp.log(tb)
+    lse_e = pe + jnp.log(te)
+    lg = (valid * (jnp.exp(le - lse_e) - jnp.exp(lb - lse_b))).astype(bf16)
+    w = lax.dot_general(lhs, lg, (((1,), (1,)), ((), ())), preferred_element_type=f32)
+    wmine[0] = jnp.sum(w[0:8], axis=0, keepdims=True)
+    wmine[1] = jnp.sum(w[8:16], axis=0, keepdims=True)
+    wcopy = send(wmine, wother, ts.at[0], tr.at[0], buddy)
+
+    pull = crr_row * valid * (meane / te - meanb / tb) / dim
+    own = lane - tk * x == sub
+    pull_col = jnp.sum(jnp.where(own, pull, 0.0), axis=1, keepdims=True)
+    own_coeff = jnp.where(x == 0, coeff[0], coeff[1])
+    ed = rows_all[z].astype(f32) + own_coeff * myval[...]
+    smine[...] = jnp.sum(pull_col * ed, axis=0, keepdims=True)
+    scopy = send(smine, sother, ts.at[1], tr.at[1], buddy)
+    kl = valid * (cross / tb - lse_b + lse_e)
+    tl = target - lse_e
+    kl_ref[...] = jnp.where(x == 0, kl, pltpu.roll(kl, tk, 1))[:, :tk]
+    tl_ref[...] = jnp.where(x == 0, tl, pltpu.roll(tl, tk, 1))[:, :tk]
+
+    wcopy.wait_recv()
+    wl = jnp.concatenate(
+        [split_rows(wmine[e] + wother[e], None) for e in range(2)], axis=0
+    ).astype(bf16)
+    back = lax.dot_general(wl, head[...], (((1,), (0,)), ((), ())), preferred_element_type=f32)
+    for e in range(2):
+        g = jnp.sum(back[e * 8 : e * 8 + 8], axis=0, keepdims=True) * gain_ref[...]
+        for s in range(nv):
+            gpart[e, s] = g[:, s * width : (s + 1) * width]
+    gall[q] = gpart[x, z]
+    gcopies = []
+    for k in range(nq - 1):
+        p = peers[k]
+        gcopies.append(send(gpart.at[p["edit"], p["vocab"]], gall.at[q], gs.at[k], gr.at[k], p))
+    scopy.wait_recv()
+    out = -(smine[...] + sother[...])
+    for d in gcopies:
+        d.wait_recv()
+    for p in range(nq):
+        out = out + gall[p]
+    grad_ref[...] = out
+    for d in list(zcopies.values()) + vcopies + ccopies + xcopies + scopies + gcopies:
+        d.wait_send()
+    wcopy.wait_send()
+    scopy.wait_send()
+
+
+def kernel_device(
+    nv, token_ids, valid_mask, key_index, hidden_act, key_table, base_out, value_vecs, norm_gain, head
+):
+    f32, bf16 = jnp.float32, jnp.bfloat16
+    tk, width = base_out.shape
+    dim = head.shape[1]
+    vrows = head.shape[0]
+    nq = nv * 2
+    dma = lambda n: pltpu.SemaphoreType.DMA((n,))
+    vmem = pl.BlockSpec(memory_space=pltpu.VMEM)
+    hbm = pl.BlockSpec(memory_space=pl.ANY)
+    smem = pl.BlockSpec(memory_space=pltpu.SMEM)
+    return pl.pallas_call(
+        functools.partial(fused, nv),
+        out_shape=(
+            jax.ShapeDtypeStruct((1, width), f32),
+            jax.ShapeDtypeStruct((1, tk), f32),
+            jax.ShapeDtypeStruct((1, tk), f32),
+        ),
+        in_specs=[smem, vmem, vmem, hbm, vmem, hbm, vmem, vmem, hbm],
+        out_specs=(vmem, vmem, vmem),
+        scratch_shapes=[
+            pltpu.VMEM(hidden_act.shape, bf16),
+            pltpu.VMEM(head.shape, bf16),
+            pltpu.VMEM((nv, tk, width), bf16),
+            pltpu.VMEM((2, nv, 1, width), f32),
+            pltpu.VMEM((1, width), f32),
+            pltpu.VMEM((2, 1, tk), f32),
+            pltpu.VMEM((nv, 2, 1, tk), f32),
+            pltpu.VMEM((4 * tk, dim), bf16),
+            pltpu.VMEM((8, 2 * tk), f32),
+            pltpu.VMEM((nq, 8, 2 * tk), f32),
+            pltpu.VMEM((2, 1, vrows), f32),
+            pltpu.VMEM((2, 1, vrows), f32),
+            pltpu.VMEM((1, width), f32),
+            pltpu.VMEM((1, width), f32),
+            pltpu.VMEM((2, nv, 1, width), f32),
+            pltpu.VMEM((nq, 1, width), f32),
+            dma(2), dma(4),
+            dma(nv), dma(nv), dma(nv), dma(nv),
+            dma(nq), dma(nq), dma(nv), dma(nv),
+            dma(nq), dma(nq), dma(nq), dma(nq),
+            dma(2), dma(2),
+        ],
+        compiler_params=pltpu.CompilerParams(
+            collective_id=0, has_side_effects=True, vmem_limit_bytes=48 * 1024 * 1024
+        ),
+    )(
+        key_index,
+        token_ids.reshape(1, tk),
+        valid_mask.reshape(1, tk),
+        hidden_act,
+        key_table,
+        base_out,
+        value_vecs,
+        norm_gain.reshape(1, dim),
+        head,
+    )
+
+
 def solution(mesh):
     placed = (
         P(("groups", "tok")),
@@ -88,8 +438,11 @@
         P(),
         P(("vocab", "edit"), None),
     )
+    body = per_device
+    if mesh.shape["edit"] == 2 and mesh.shape["tok"] == 2 and 3 <= mesh.shape["vocab"] <= 4:
+        body = functools.partial(kernel_device, mesh.shape["vocab"])
     return jax.shard_map(
-        per_device,
+        body,
         mesh=mesh,
         in_specs=placed,
         out_specs=(

time: 156 us -> 41 us (0.26)
  blocking collectives: 140 us -> 0 us
  Pallas kernels: 0 us -> 30.1 us
  matrix products: 10 us -> 0 us
  local copies, waits for them, and re-layouts: 1.73 us -> 9.83 us
  other arithmetic: 3.51 us -> 0 us
    psum x3 -> x0, blocking collectives: 88.7 us -> none  [the longest x1 57.6 us: per_device(): grad_total = lax.psum(grad_part, ('vocab', 'edit', 'tok'))]
    all_gather x3 -> x0, blocking collectives: 32.6 us -> none  [the longest x1 15 us: per_device(): lax.all_gather(base_out, 'vocab', axis=1, tiled=True)]
    pallas_call x0 -> x1, Pallas kernels: none -> 30.1 us  [kernel_device(): pl.pallas_call(functools.partial(fused, nv), out_shape=(jax.ShapeDtypeStr...]
    pmax x1 -> x0, blocking collectives: 18.6 us -> none  [per_device(): peak_base, peak_edit = lax.pmax((peak_base, peak_edit), ('vocab', 'edit'))]
    dot_general x4 -> x0, matrix products: 10 us -> none  [the longest x1 3.87 us: per_device(): lax.dot_general(base_norm, head, (((1,), (1,)), ((), ())), preferred_elem...]
    unnamed x7 -> x21, local copies, waits for them, and re-layouts: 0.53 us -> 9.83 us
    reduce_sum x5 -> x0, other arithmetic: 1.85 us -> none  [the longest x1 0.81 us: per_device(): grad_part = jnp.sum(coeff[:, :, None] * grad_o, axis=1)]
where the time goes in v1:
time: 41 us; the launch traced here: 40.6 us
  Pallas kernels  30.1 us (73%)
  local copies, waits for them, and re-layouts  9.83 us (24%)
  between operations  0.66 us (2%)
    pallas_call x1, Pallas kernels, kernel_device(): pl.pallas_call(functools.partial(fused, nv), out_shape=(jax.ShapeDtypeStr...  30.1 us
    unnamed x21, local copies, waits for them, and re-layouts  9.83 us

profile of v1, /device:TPU:0, one launch (start us, length us, event | category | flops | bytes accessed | tf_op | source)
XLA Modules:
  0.0 40.6 jit_solution(12980288090932415447)
XLA Ops:
  0.6 0.0 copy-start
  0.6 2.2 %copy-done = bf16[512,4096]{1,0:T(8,128)(2,1)S(1)} copy-done((bf16[512,4096]{1,0:T(8,128)(2,1)S(1)}, bf16[512,4096]{1,0:T(8,128)(2,1)}, u32[]{:S(2)}) %copy-start) | copy-done | bytes 4194328
  2.8 0.0 copy-start.1
  2.8 1.0 %copy-done.1 = bf16[64,3584]{1,0:T(8,128)(2,1)S(1)} copy-done((bf16[64,3584]{1,0:T(8,128)(2,1)S(1)}, bf16[64,3584]{1,0:T(8,128)(2,1)}, u32[]{:S(2)}) %copy-start.1) | copy-done | bytes 458776
  3.8 0.0 copy-start.2
  3.8 0.9 %copy-done.2 = bf16[64,1024]{1,0:T(8,128)(2,1)S(1)} copy-done((bf16[64,1024]{1,0:T(8,128)(2,1)S(1)}, bf16[64,1024]{1,0:T(8,128)(2,1)}, u32[]{:S(2)}) %copy-start.2) | copy-done | bytes 131096
  4.7 0.0 copy-start.3
  4.7 0.7 %copy-done.3 = bf16[4,3584]{1,0:T(4,128)(2,1)S(1)} copy-done((bf16[4,3584]{1,0:T(4,128)(2,1)S(1)}, bf16[4,3584]{1,0:T(4,128)(2,1)}, u32[]{:S(2)}) %copy-start.3) | copy-done | bytes 28696
  5.5 0.0 copy-start.4
  5.5 0.7 %copy-done.4 = f32[4096]{0:T(1024)S(1)} copy-done((f32[4096]{0:T(1024)S(1)}, f32[4096]{0:T(1024)}, u32[]{:S(2)}) %copy-start.4) | copy-done | bytes 16408
  6.2 0.0 copy-start.5
  6.2 0.7 %copy-done.5 = bf16[1,1024]{1,0:T(2,128)(2,1)S(1)} copy-done((bf16[1,1024]{1,0:T(2,128)(2,1)S(1)}, bf16[1,1024]{1,0:T(2,128)(2,1)}, u32[]{:S(2)}) %copy-start.5) | copy-done | bytes 2072
  6.9 0.0 copy-start.6
  6.9 0.7 %copy-done.6 = s32[2]{0:T(128)S(1)} copy-done((s32[2]{0:T(128)S(1)}, s32[2]{0:T(128)}, u32[]{:S(2)}) %copy-start.6) | copy-done | bytes 32
  7.6 0.0 copy-start.7
  7.6 0.7 %copy-done.7 = s32[64]{0:T(128)S(1)} copy-done((s32[64]{0:T(128)S(1)}, s32[64]{0:T(128)}, u32[]{:S(2)}) %copy-start.7) | copy-done | bytes 280
  8.2 0.0 copy-start.8
  8.2 0.7 %copy-done.8 = s32[64]{0:T(128)S(1)} copy-done((s32[64]{0:T(128)S(1)}, s32[64]{0:T(128)}, u32[]{:S(2)}) %copy-start.8) | copy-done | bytes 280
  8.9 30.1 %shard_map.112 = (f32[1,1024]{1,0:T(1,128)S(1)}, f32[1,64]{1,0:T(1,128)S(1)}, f32[1,64]{1,0:T(1,128)S(1)}) custom-call(s32[2]{0:T(128)S(1)} %copy-done.6, s32[1,64]{1,0:T(1,128)S(1)} %bitcast.4, s32[1,64]{1,0:T(1,128)S(1)} %bitcast.5, bf16[64,3584]{1,0:T(8,128)(2,1)S(1)} %copy-done.1, bf16[4,3584]{1,0:T(4,128)(2,1)S(1)} %copy-done.3, ...), custom_call_target="tpu_custom_call" | custom-call | tf_op jit(solution)/shard_map/pallas_call | solution.py:381
  38.9 0.6 %copy.15 = f32[1,1024]{1,0:T(1,128)} copy(f32[1,1024]{1,0:T(1,128)S(1)} %get-tuple-element.6) | data formatting | bytes 8192
  39.5 0.5 %copy.16 = f32[1,64]{1,0:T(1,128)} copy(f32[1,64]{1,0:T(1,128)S(1)} %get-tuple-element.7) | data formatting | bytes 512
  40.0 0.5 %copy.17 = f32[1,64]{1,0:T(1,128)} copy(f32[1,64]{1,0:T(1,128)S(1)} %get-tuple-element.8) | data formatting | bytes 512
Async XLA Ops:
  0.6 2.2 %copy-start = (bf16[512,4096]{1,0:T(8,128)(2,1)S(1)}, bf16[512,4096]{1,0:T(8,128)(2,1)}, u32[]{:S(2)}) copy-start(bf16[512,4096]{1,0:T(8,128)(2,1)} %head_hbm.1) | copy-start | bytes 12582916
  2.8 1.0 %copy-start.1 = (bf16[64,3584]{1,0:T(8,128)(2,1)S(1)}, bf16[64,3584]{1,0:T(8,128)(2,1)}, u32[]{:S(2)}) copy-start(bf16[64,3584]{1,0:T(8,128)(2,1)} %act_hbm.1) | copy-start | bytes 1376260
  3.8 0.9 %copy-start.2 = (bf16[64,1024]{1,0:T(8,128)(2,1)S(1)}, bf16[64,1024]{1,0:T(8,128)(2,1)}, u32[]{:S(2)}) copy-start(bf16[64,1024]{1,0:T(8,128)(2,1)} %base_hbm.1) | copy-start | bytes 393220
  4.7 0.7 %copy-start.3 = (bf16[4,3584]{1,0:T(4,128)(2,1)S(1)}, bf16[4,3584]{1,0:T(4,128)(2,1)}, u32[]{:S(2)}) copy-start(bf16[4,3584]{1,0:T(4,128)(2,1)} %table_ref.1) | copy-start | bytes 86020
  5.5 0.7 %copy-start.4 = (f32[4096]{0:T(1024)S(1)}, f32[4096]{0:T(1024)}, u32[]{:S(2)}) copy-start(f32[4096]{0:T(1024)} %param.16) | copy-start | bytes 49156
  6.2 0.7 %copy-start.5 = (bf16[1,1024]{1,0:T(2,128)(2,1)S(1)}, bf16[1,1024]{1,0:T(2,128)(2,1)}, u32[]{:S(2)}) copy-start(bf16[1,1024]{1,0:T(2,128)(2,1)} %val_ref.1) | copy-start | bytes 6148
  6.9 0.7 %copy-start.6 = (s32[2]{0:T(128)S(1)}, s32[2]{0:T(128)}, u32[]{:S(2)}) copy-start(s32[2]{0:T(128)} %key_ref.1) | copy-start | bytes 28
  7.6 0.7 %copy-start.7 = (s32[64]{0:T(128)S(1)}, s32[64]{0:T(128)}, u32[]{:S(2)}) copy-start(s32[64]{0:T(128)} %param.9) | copy-start | bytes 772
  8.2 0.7 %copy-start.8 = (s32[64]{0:T(128)S(1)}, s32[64]{0:T(128)}, u32[]{:S(2)}) copy-start(s32[64]{0:T(128)} %param.10) | copy-start | bytes 772

commit v2 on v1

--- a/solution.py
+++ b/solution.py
@@ -95,18 +95,24 @@
 
 def fused(
     nv,
-    key_ref,
-    ids_ref,
-    mask_ref,
+    key_hbm,
+    ids_hbm,
+    mask_hbm,
     act_hbm,
-    table_ref,
+    table_hbm,
     base_hbm,
-    val_ref,
-    gain_ref,
+    val_hbm,
+    gain_hbm,
     head_hbm,
     grad_ref,
     kl_ref,
     tl_ref,
+    key_ref,
+    ids_ref,
+    mask_ref,
+    table_ref,
+    val_ref,
+    gain_ref,
     act,
     head,
     rows_all,
@@ -114,6 +120,9 @@
     myval,
     cpart,
     call,
+    sqpart,
+    sqall,
+    acc,
     normed,
     stat,
     stats,
@@ -124,7 +133,6 @@
     gpart,
     gall,
     local_sem,
-    head_sem,
     zs,
     zr,
     xs,
@@ -133,6 +141,8 @@
     vr,
     cs,
     cr,
+    qs,
+    qr,
     ss,
     sr,
     gs,
@@ -148,7 +158,7 @@
     nq = nv * 2
     tk, width = base_hbm.shape
     half = tk // 2
-    dim = gain_ref.shape[1]
+    dim = gain_hbm.shape[1]
     vrows = head_hbm.shape[0]
     hv = vrows // 4
 
@@ -162,18 +172,25 @@
         pl.semaphore_signal(barrier, inc=1, device_id=p, device_id_type=MESH)
     pl.semaphore_signal(barrier, inc=1, device_id=buddy, device_id_type=MESH)
 
-    base_in = pltpu.make_async_copy(base_hbm, rows_all.at[z], local_sem.at[0])
-    base_in.start()
-    act_in = pltpu.make_async_copy(act_hbm, act, local_sem.at[1])
-    act_in.start()
+    def fetch(src, dst, i):
+        d = pltpu.make_async_copy(src, dst, local_sem.at[i])
+        d.start()
+        return d
+
+    val_in = fetch(val_hbm, val_ref, 0)
+    base_in = fetch(base_hbm, rows_all.at[z], 1)
+    small_in = [
+        fetch(key_hbm, key_ref, 2),
+        fetch(table_hbm, table_ref, 3),
+        fetch(act_hbm, act, 4),
+        fetch(ids_hbm, ids_ref, 5),
+        fetch(mask_hbm, mask_ref, 6),
+        fetch(gain_hbm, gain_ref, 7),
+    ]
     head_in = [
-        pltpu.make_async_copy(
-            head_hbm.at[pl.ds(i * hv, hv)], head.at[pl.ds(i * hv, hv)], head_sem.at[i]
-        )
-        for i in range(4)
+        fetch(head_hbm.at[pl.ds(i * hv, hv)], head.at[pl.ds(i * hv, hv)], 8 + i) for i in range(4)
     ]
-    for d in head_in:
-        d.start()
+    val_in.wait()
     myval[...] = val_ref[...].astype(f32)
     vals[x, z] = myval[...]
     base_in.wait()
@@ -188,28 +205,26 @@
         d.start()
         return d
 
+    vcopies = [
+        send(myval, vals.at[x, z], vs.at[k], vr.at[k], peers[k]) for k in range(nq - 1)
+    ]
     order = [1, nv - 1] + [k for k in range(2, nv - 1)]
     zcopies = {}
     for k in order:
         zcopies[k] = send(
             rows_all.at[z, mine], rows_all.at[z, mine], zs.at[k], zr.at[k], {"vocab": lax.rem(z + k, nv)}
         )
-    vcopies = [
-        send(myval, vals.at[x, z], vs.at[k], vr.at[k], peers[k]) for k in range(nq - 1)
-    ]
-
-    act_in.wait()
+
+    for d in small_in:
+        d.wait()
     every = lax.dot_general(
         table_ref[...], act[...], (((1,), (1,)), ((), ())), preferred_element_type=f32
     )
-    picked = []
+    slots = lax.broadcasted_iota(jnp.int32, every.shape, 0)
     for e in range(2):
-        one = jnp.zeros((1, tk), f32)
-        for k in range(every.shape[0]):
-            one = one + jnp.where(key_ref[e] == k, every[k : k + 1, :], 0.0)
-        picked.append(one)
-    for e in range(2):
-        cpart[e] = picked[e]
+        cpart[e] = jnp.sum(
+            jnp.where(slots == key_ref[:, e : e + 1], every, 0.0), axis=0, keepdims=True
+        )
     call[z] = cpart[...]
     ccopies = [
         send(cpart, call.at[z], cs.at[k], cr.at[k], {"vocab": lax.rem(z + k, nv)})
@@ -237,15 +252,6 @@
     valid_col = to_col(mask_ref[...].astype(f32))
     valid = to_row(valid_col, valid_col)
 
-    xcopies = []
-    for k in order:
-        zcopies[k].wait_recv()
-        s = lax.rem(z - k + nv, nv)
-        xcopies.append(
-            send(
-                rows_all.at[s, mine], rows_all.at[s, mine], xs.at[k], xr.at[k], {"edit": 1 - x}
-            )
-        )
     for d in ccopies:
         d.wait_recv()
     for d in vcopies:
@@ -256,32 +262,65 @@
         for s in range(1, nv):
             total = total + call[s, e]
         coeff.append(to_col(total))
-    for d in xcopies:
+    b = rows_all[z].astype(f32)
+    sq = [jnp.sum(b * b, axis=1, keepdims=True)]
+    for e in range(2):
+        ed = b + coeff[e] * vals[e, z]
+        sq.append(jnp.sum(ed * ed, axis=1, keepdims=True))
+    sqpart[0] = to_row(sq[0], sq[0])
+    sqpart[1] = to_row(sq[1], sq[2])
+    sqall[z] = sqpart[...]
+    qcopies = [
+        send(sqpart, sqall.at[z], qs.at[k], qr.at[k], {"vocab": lax.rem(z + k, nv)})
+        for k in range(1, nv)
+    ]
+    xcopies = {}
+    for k in order:
+        zcopies[k].wait_recv()
+        s = lax.rem(z - k + nv, nv)
+        xcopies[k] = send(
+            rows_all.at[s, mine], rows_all.at[s, mine], xs.at[k], xr.at[k], {"edit": 1 - x}
+        )
+    for d in qcopies:
         d.wait_recv()
-
-    sq = [jnp.zeros((tk, 1), f32) for _ in range(3)]
-    for s in range(nv):
-        b = rows_all[s].astype(f32)
-        sq[0] = sq[0] + jnp.sum(b * b, axis=1, keepdims=True)
-        for e in range(2):
-            ed = b + coeff[e] * vals[e, s]
-            sq[1 + e] = sq[1 + e] + jnp.sum(ed * ed, axis=1, keepdims=True)
-    scale = [lax.rsqrt(t / dim + NORM_EPS) for t in sq]
-    for s in range(nv):
-        cols = pl.ds(s * width, width)
+    sqb, sqe = sqall[0, 0], sqall[0, 1]
+    for s in range(1, nv):
+        sqb = sqb + sqall[s, 0]
+        sqe = sqe + sqall[s, 1]
+    rb_row = lax.rsqrt(sqb / dim + NORM_EPS)
+    re_row = lax.rsqrt(sqe / dim + NORM_EPS)
+    c_row = to_row(coeff[0], coeff[1])
+    in0 = lane == sub
+    in1 = lane == sub + tk
+
+    def col_of(where, row):
+        return jnp.sum(jnp.where(where, row, 0.0), axis=1, keepdims=True)
+
+    scale = [col_of(in0, rb_row), col_of(in0, re_row), col_of(in1, re_row)]
+    for step, k in enumerate([0] + order):
+        if step == 0:
+            for d in head_in:
+                d.wait()
+        else:
+            xcopies[k].wait_recv()
+        s = lax.rem(z - k + nv, nv)
+        cols = pl.ds(pl.multiple_of(s * width, width), width)
         b = rows_all[s].astype(f32)
         gain = gain_ref[:, cols]
         plain = (gain * b * scale[0]).astype(bf16)
-        normed[0:tk, cols] = plain
-        normed[tk : 2 * tk, cols] = plain
+        normed[step, 0:tk] = plain
+        normed[step, tk : 2 * tk] = plain
         for e in range(2):
             ed = b + coeff[e] * vals[e, s]
-            normed[(2 + e) * tk : (3 + e) * tk, cols] = (gain * ed * scale[1 + e]).astype(bf16)
-    for d in head_in:
-        d.wait()
-    logit = lax.dot_general(
-        head[...], normed[...], (((1,), (1,)), ((), ())), preferred_element_type=f32
-    )
+            normed[step, (2 + e) * tk : (3 + e) * tk] = (gain * ed * scale[1 + e]).astype(bf16)
+        part = lax.dot_general(
+            head[:, cols], normed[step], (((1,), (1,)), ((), ())), preferred_element_type=f32
+        )
+        if step == 0:
+            acc[...] = part
+        else:
+            acc[...] += part
+    logit = acc[...]
     lb, le = logit[:, : 2 * tk], logit[:, 2 * tk :]
     vid = (q * vrows + lax.broadcasted_iota(jnp.int32, lb.shape, 0)).astype(f32)
     mb = jnp.max(lb, axis=0, keepdims=True)
@@ -298,8 +337,8 @@
     stat[7:8] = jnp.sum(jnp.where(vid == ids_row, le, 0.0), axis=0, keepdims=True)
     stats[q] = stat[...]
     scopies = [send(stat, stats.at[q], ss.at[k], sr.at[k], peers[k]) for k in range(nq - 1)]
-    cr_row = to_row(coeff[0] * scale[1], coeff[1] * scale[2])
-    crr_row = to_row(coeff[0] * scale[1] * scale[1], coeff[1] * scale[2] * scale[2])
+    cr_row = c_row * re_row
+    crr_row = cr_row * re_row
     lanes8 = lax.broadcasted_iota(jnp.int32, (8, 2 * tk), 1)
     lhs = jnp.concatenate(
         [split_rows(cr_row, lanes8 < tk), split_rows(cr_row, lanes8 >= tk)], axis=0
@@ -360,7 +399,7 @@
     for p in range(nq):
         out = out + gall[p]
     grad_ref[...] = out
-    for d in list(zcopies.values()) + vcopies + ccopies + xcopies + scopies + gcopies:
+    for d in list(zcopies.values()) + list(xcopies.values()) + vcopies + ccopies + qcopies + scopies + gcopies:
         d.wait_send()
     wcopy.wait_send()
     scopy.wait_send()
@@ -376,8 +415,7 @@
     nq = nv * 2
     dma = lambda n: pltpu.SemaphoreType.DMA((n,))
     vmem = pl.BlockSpec(memory_space=pltpu.VMEM)
-    hbm = pl.BlockSpec(memory_space=pl.ANY)
-    smem = pl.BlockSpec(memory_space=pltpu.SMEM)
+    hbm = pl.BlockSpec(memory_space=pltpu.HBM)
     return pl.pallas_call(
         functools.partial(fused, nv),
         out_shape=(
@@ -385,9 +423,15 @@
             jax.ShapeDtypeStruct((1, tk), f32),
             jax.ShapeDtypeStruct((1, tk), f32),
         ),
-        in_specs=[smem, vmem, vmem, hbm, vmem, hbm, vmem, vmem, hbm],
+        in_specs=[hbm] * 9,
         out_specs=(vmem, vmem, vmem),
         scratch_shapes=[
+            pltpu.VMEM((1, 2), jnp.int32),
+            pltpu.VMEM((1, tk), jnp.int32),
+            pltpu.VMEM((1, tk), jnp.int32),
+            pltpu.VMEM(key_table.shape, bf16),
+            pltpu.VMEM((1, width), bf16),
+            pltpu.VMEM((1, dim), f32),
             pltpu.VMEM(hidden_act.shape, bf16),
             pltpu.VMEM(head.shape, bf16),
             pltpu.VMEM((nv, tk, width), bf16),
@@ -395,7 +439,10 @@
             pltpu.VMEM((1, width), f32),
             pltpu.VMEM((2, 1, tk), f32),
             pltpu.VMEM((nv, 2, 1, tk), f32),
-            pltpu.VMEM((4 * tk, dim), bf16),
+            pltpu.VMEM((2, 1, 2 * tk), f32),
+            pltpu.VMEM((nv, 2, 1, 2 * tk), f32),
+            pltpu.VMEM((vrows, 4 * tk), f32),
+            pltpu.VMEM((nv, 4 * tk, width), bf16),
             pltpu.VMEM((8, 2 * tk), f32),
             pltpu.VMEM((nq, 8, 2 * tk), f32),
             pltpu.VMEM((2, 1, vrows), f32),
@@ -404,17 +451,17 @@
             pltpu.VMEM((1, width), f32),
             pltpu.VMEM((2, nv, 1, width), f32),
             pltpu.VMEM((nq, 1, width), f32),
-            dma(2), dma(4),
+            dma(12),
             dma(nv), dma(nv), dma(nv), dma(nv),
-            dma(nq), dma(nq), dma(nv), dma(nv),
+            dma(nq), dma(nq), dma(nv), dma(nv), dma(nv), dma(nv),
             dma(nq), dma(nq), dma(nq), dma(nq),
             dma(2), dma(2),
         ],
         compiler_params=pltpu.CompilerParams(
-            collective_id=0, has_side_effects=True, vmem_limit_bytes=48 * 1024 * 1024
+            collective_id=0, has_side_effects=True, vmem_limit_bytes=64 * 1024 * 1024
         ),
     )(
-        key_index,
+        key_index.reshape(1, 2),
         token_ids.reshape(1, tk),
         valid_mask.reshape(1, tk),
         hidden_act,

time: 41 us -> 36.2 us (0.88)
  local copies, waits for them, and re-layouts: 9.83 us -> 3.58 us
  Pallas kernels: 30.1 us -> 31.7 us
    unnamed x21 -> x3, local copies, waits for them, and re-layouts: 9.83 us -> 3.58 us
    pallas_call x1, Pallas kernels: 30.1 us -> 31.7 us  [kernel_device(): pl.pallas_call(functools.partial(fused, nv), out_shape=(jax.ShapeDtypeStr...]
where the time goes in v2:
time: 36.2 us; the launch traced here: 35.9 us
  Pallas kernels  31.7 us (88%)
  local copies, waits for them, and re-layouts  3.58 us (10%)
  between operations  0.64 us (2%)
    pallas_call x1, Pallas kernels, kernel_device(): pl.pallas_call(functools.partial(fused, nv), out_shape=(jax.ShapeDtypeStr...  31.7 us
    unnamed x3, local copies, waits for them, and re-layouts  3.58 us

profile of v2, /device:TPU:0, one launch (start us, length us, event | category | flops | bytes accessed | tf_op | source)
XLA Modules:
  0.0 35.9 jit_solution(12382251022867187646)
XLA Ops:
  0.6 31.7 %shard_map.112 = (f32[1,1024]{1,0:T(1,128)}, f32[1,64]{1,0:T(1,128)}, f32[1,64]{1,0:T(1,128)}) custom-call(s32[1,2]{1,0:T(1,128)} %bitcast.5, s32[1,64]{1,0:T(1,128)} %bitcast.6, s32[1,64]{1,0:T(1,128)} %bitcast.7, bf16[64,3584]{1,0:T(8,128)(2,1)} %act_hbm.1, bf16[4,3584]{1,0:T(4,128)(2,1)} %table_hbm.1, bf16[64,1024]{1,0:T(8,128)(2,1)} %base_hbm.1, ...), custom_call_target="tpu_custom_call" | custom-call | tf_op jit(solution)/shard_map/pallas_call | solution.py:419
  32.3 1.3 %copy.15 = f32[1,1024]{1,0:T(1,128)} copy(f32[1,1024]{1,0:T(1,128)} %get-tuple-element.6) | data formatting | bytes 8192
  33.6 1.1 %copy.16 = f32[1,64]{1,0:T(1,128)} copy(f32[1,64]{1,0:T(1,128)} %get-tuple-element.7) | data formatting | bytes 512
  34.7 1.2 %copy.17 = f32[1,64]{1,0:T(1,128)} copy(f32[1,64]{1,0:T(1,128)} %get-tuple-element.8) | data formatting | bytes 512

commit v3 on v2

--- a/solution.py
+++ b/solution.py
@@ -134,6 +134,7 @@
     gall,
     local_sem,
     zs,
+    zf,
     zr,
     xs,
     xr,
@@ -194,27 +195,6 @@
     myval[...] = val_ref[...].astype(f32)
     vals[x, z] = myval[...]
     base_in.wait()
-    pl.semaphore_wait(barrier, nq)
-
-    mine = pl.ds(pl.multiple_of(x * half, half), half)
-
-    def send(src, dst, ssem, rsem, dev):
-        d = pltpu.make_async_remote_copy(
-            src_ref=src, dst_ref=dst, send_sem=ssem, recv_sem=rsem, device_id=dev, device_id_type=MESH
-        )
-        d.start()
-        return d
-
-    vcopies = [
-        send(myval, vals.at[x, z], vs.at[k], vr.at[k], peers[k]) for k in range(nq - 1)
-    ]
-    order = [1, nv - 1] + [k for k in range(2, nv - 1)]
-    zcopies = {}
-    for k in order:
-        zcopies[k] = send(
-            rows_all.at[z, mine], rows_all.at[z, mine], zs.at[k], zr.at[k], {"vocab": lax.rem(z + k, nv)}
-        )
-
     for d in small_in:
         d.wait()
     every = lax.dot_general(
@@ -226,15 +206,70 @@
             jnp.where(slots == key_ref[:, e : e + 1], every, 0.0), axis=0, keepdims=True
         )
     call[z] = cpart[...]
+    pl.semaphore_wait(barrier, nq)
+
+    quarter = half // 2
+
+    def piece(h, sub):
+        return pl.ds(pl.multiple_of(h * half + sub * quarter, quarter), quarter)
+
+    def remote(src, dst, ssem, rsem, dev):
+        return pltpu.make_async_remote_copy(
+            src_ref=src, dst_ref=dst, send_sem=ssem, recv_sem=rsem, device_id=dev, device_id_type=MESH
+        )
+
+    def send(src, dst, ssem, rsem, dev):
+        d = remote(src, dst, ssem, rsem, dev)
+        d.start()
+        return d
+
+    def along(s, sub, ssem, to):
+        ref = rows_all.at[s, piece(x, sub)]
+        return remote(ref, ref, ssem, zr.at[s * 2 + sub], {"vocab": to})
+
+    def across(s, h, sub, ssem):
+        ref = rows_all.at[s, piece(h, sub)]
+        return remote(ref, ref, ssem, xr.at[s * 2 + sub], {"edit": 1 - x})
+
+    first_s = z + 1 - 2 * ((z + 3) // 4)
+    third_s = 3 * (1 - z // 2)
+    steps = [first_s, 6 - z - first_s - third_s, third_s]
+    onward = [z + 1, z - 1, 3 * z - 3]
+    middle = z * (3 - z) > 0
+    for sub in range(2):
+
+        @pl.when(z < nv - 1)
+        def _():
+            along(z, sub, zs.at[sub], z + 1).start()
+
+        @pl.when(z > 0)
+        def _():
+            along(z, sub, zs.at[2 + sub], z - 1).start()
+
     ccopies = [
         send(cpart, call.at[z], cs.at[k], cr.at[k], {"vocab": lax.rem(z + k, nv)})
         for k in range(1, nv)
     ]
 
-    sub = lax.broadcasted_iota(jnp.int32, (tk, 2 * tk), 0)
+    vcopies = [
+        send(myval, vals.at[x, z], vs.at[k], vr.at[k], peers[k]) for k in range(nq - 1)
+    ]
+
+    def pass_on(i):
+        for sub in range(2):
+            at = i * 2 + sub
+            along(steps[i], sub, zf.at[at], z).wait_recv()
+
+            @pl.when(middle)
+            def _():
+                along(steps[i], sub, zf.at[at], onward[i]).start()
+
+            across(steps[i], x, sub, xs.at[at]).start()
+
+    row_at = lax.broadcasted_iota(jnp.int32, (tk, 2 * tk), 0)
     lane = lax.broadcasted_iota(jnp.int32, (tk, 2 * tk), 1)
     first = lane < tk
-    diag = jnp.where(first, lane, lane - tk) == sub
+    diag = jnp.where(first, lane, lane - tk) == row_at
     eye = lax.broadcasted_iota(jnp.int32, (tk, tk), 0) == lax.broadcasted_iota(
         jnp.int32, (tk, tk), 1
     )
@@ -252,6 +287,7 @@
     valid_col = to_col(mask_ref[...].astype(f32))
     valid = to_row(valid_col, valid_col)
 
+    pass_on(0)
     for d in ccopies:
         d.wait_recv()
     for d in vcopies:
@@ -274,13 +310,8 @@
         send(sqpart, sqall.at[z], qs.at[k], qr.at[k], {"vocab": lax.rem(z + k, nv)})
         for k in range(1, nv)
     ]
-    xcopies = {}
-    for k in order:
-        zcopies[k].wait_recv()
-        s = lax.rem(z - k + nv, nv)
-        xcopies[k] = send(
-            rows_all.at[s, mine], rows_all.at[s, mine], xs.at[k], xr.at[k], {"edit": 1 - x}
-        )
+    pass_on(1)
+    pass_on(2)
     for d in qcopies:
         d.wait_recv()
     sqb, sqe = sqall[0, 0], sqall[0, 1]
@@ -290,20 +321,21 @@
     rb_row = lax.rsqrt(sqb / dim + NORM_EPS)
     re_row = lax.rsqrt(sqe / dim + NORM_EPS)
     c_row = to_row(coeff[0], coeff[1])
-    in0 = lane == sub
-    in1 = lane == sub + tk
+    in0 = lane == row_at
+    in1 = lane == row_at + tk
 
     def col_of(where, row):
         return jnp.sum(jnp.where(where, row, 0.0), axis=1, keepdims=True)
 
     scale = [col_of(in0, rb_row), col_of(in0, re_row), col_of(in1, re_row)]
-    for step, k in enumerate([0] + order):
+    for step in range(nv):
         if step == 0:
             for d in head_in:
                 d.wait()
         else:
-            xcopies[k].wait_recv()
-        s = lax.rem(z - k + nv, nv)
+            for sub in range(2):
+                across(steps[step - 1], 1 - x, sub, xs.at[0]).wait_recv()
+        s = z if step == 0 else steps[step - 1]
         cols = pl.ds(pl.multiple_of(s * width, width), width)
         b = rows_all[s].astype(f32)
         gain = gain_ref[:, cols]
@@ -367,7 +399,7 @@
     wcopy = send(wmine, wother, ts.at[0], tr.at[0], buddy)
 
     pull = crr_row * valid * (meane / te - meanb / tb) / dim
-    own = lane - tk * x == sub
+    own = lane - tk * x == row_at
     pull_col = jnp.sum(jnp.where(own, pull, 0.0), axis=1, keepdims=True)
     own_coeff = jnp.where(x == 0, coeff[0], coeff[1])
     ed = rows_all[z].astype(f32) + own_coeff * myval[...]
@@ -399,10 +431,39 @@
     for p in range(nq):
         out = out + gall[p]
     grad_ref[...] = out
-    for d in list(zcopies.values()) + list(xcopies.values()) + vcopies + ccopies + qcopies + scopies + gcopies:
+    for sub in range(2):
+
+        @pl.when(z < nv - 1)
+        def _():
+            along(z, sub, zs.at[sub], z + 1).wait_send()
+
+        @pl.when(z > 0)
+        def _():
+            along(z, sub, zs.at[2 + sub], z - 1).wait_send()
+
+        for i in range(3):
+
+            @pl.when(middle)
+            def _():
+                along(steps[i], sub, zf.at[i * 2 + sub], onward[i]).wait_send()
+
+            across(steps[i], x, sub, xs.at[i * 2 + sub]).wait_send()
+
+    for d in vcopies + ccopies + qcopies + scopies + gcopies:
         d.wait_send()
     wcopy.wait_send()
     scopy.wait_send()
+
+
+def hand_out(a_ref, b_ref, c_ref, a_out, b_out, c_out, sem):
+    moves = [
+        pltpu.make_async_copy(src, dst, sem.at[i])
+        for i, (src, dst) in enumerate(((a_ref, a_out), (b_ref, b_out), (c_ref, c_out)))
+    ]
+    for d in moves:
+        d.start()
+    for d in moves:
+        d.wait()
 
 
 def kernel_device(
@@ -416,13 +477,14 @@
     dma = lambda n: pltpu.SemaphoreType.DMA((n,))
     vmem = pl.BlockSpec(memory_space=pltpu.VMEM)
     hbm = pl.BlockSpec(memory_space=pltpu.HBM)
-    return pl.pallas_call(
+    shapes = (
+        jax.ShapeDtypeStruct((1, width), f32),
+        jax.ShapeDtypeStruct((1, tk), f32),
+        jax.ShapeDtypeStruct((1, tk), f32),
+    )
+    parts = pl.pallas_call(
         functools.partial(fused, nv),
-        out_shape=(
-            jax.ShapeDtypeStruct((1, width), f32),
-            jax.ShapeDtypeStruct((1, tk), f32),
-            jax.ShapeDtypeStruct((1, tk), f32),
-        ),
+        out_shape=shapes,
         in_specs=[hbm] * 9,
         out_specs=(vmem, vmem, vmem),
         scratch_shapes=[
@@ -452,7 +514,7 @@
             pltpu.VMEM((2, nv, 1, width), f32),
             pltpu.VMEM((nq, 1, width), f32),
             dma(12),
-            dma(nv), dma(nv), dma(nv), dma(nv),
+            dma(4), dma(6), dma(2 * nv), dma(6), dma(2 * nv),
             dma(nq), dma(nq), dma(nv), dma(nv), dma(nv), dma(nv),
             dma(nq), dma(nq), dma(nq), dma(nq),
             dma(2), dma(2),
@@ -471,6 +533,13 @@
         norm_gain.reshape(1, dim),
         head,
     )
+    return pl.pallas_call(
+        hand_out,
+        out_shape=shapes,
+        in_specs=[hbm] * 3,
+        out_specs=(hbm,) * 3,
+        scratch_shapes=[dma(3)],
+    )(*parts)
 
 
 def solution(mesh):
@@ -486,7 +555,7 @@
         P(("vocab", "edit"), None),
     )
     body = per_device
-    if mesh.shape["edit"] == 2 and mesh.shape["tok"] == 2 and 3 <= mesh.shape["vocab"] <= 4:
+    if mesh.shape["edit"] == 2 and mesh.shape["tok"] == 2 and mesh.shape["vocab"] == 4:
         body = functools.partial(kernel_device, mesh.shape["vocab"])
     return jax.shard_map(
         body,

time: 36.2 us -> 34.3 us (0.948)
  local copies, waits for them, and re-layouts: 3.58 us -> 0 us
  Pallas kernels: 31.7 us -> 33.5 us
    unnamed x3 -> x0, local copies, waits for them, and re-layouts: 3.58 us -> none
    pallas_call x1 -> x2, Pallas kernels: 31.7 us -> 33.5 us  [the longest x1 32.2 us: kernel_device(): pl.pallas_call(functools.partial(fused, nv), out_shape=shapes, in_specs=[...]
where the time goes in v3:
time: 34.3 us; the launch traced here: 34.2 us
  Pallas kernels  33.5 us (98%)
  between operations  0.64 us (2%)
    pallas_call x1, Pallas kernels, kernel_device(): pl.pallas_call(functools.partial(fused, nv), out_shape=shapes, in_specs=[...  32.2 us
    pallas_call x1, Pallas kernels, kernel_device(): pl.pallas_call(hand_out, out_shape=shapes, in_specs=[hbm] * 3, out_specs=...  1.29 us

profile of v3, /device:TPU:0, one launch (start us, length us, event | category | flops | bytes accessed | tf_op | source)
XLA Modules:
  0.0 34.2 jit_solution(6162687607882668648)
XLA Ops:
  0.6 32.2 %shard_map.112 = (f32[1,1024]{1,0:T(1,128)}, f32[1,64]{1,0:T(1,128)}, f32[1,64]{1,0:T(1,128)}) custom-call(s32[1,2]{1,0:T(1,128)} %bitcast.5, s32[1,64]{1,0:T(1,128)} %bitcast.6, s32[1,64]{1,0:T(1,128)} %bitcast.7, bf16[64,3584]{1,0:T(8,128)(2,1)} %act_hbm.1, bf16[4,3584]{1,0:T(4,128)(2,1)} %table_hbm.1, bf16[64,1024]{1,0:T(8,128)(2,1)} %base_hbm.1, ...), custom_call_target="tpu_custom_call" | custom-call | tf_op jit(solution)/shard_map/pallas_call | solution.py:485
  32.9 1.3 %shard_map.113 = (f32[1,1024]{1,0:T(1,128)}, f32[1,64]{1,0:T(1,128)}, f32[1,64]{1,0:T(1,128)}) custom-call(f32[1,1024]{1,0:T(1,128)} %get-tuple-element.6.a_ref, f32[1,64]{1,0:T(1,128)} %get-tuple-element.7.b_ref, f32[1,64]{1,0:T(1,128)} %get-tuple-element.8.c_ref), custom_call_target="tpu_custom_call" | custom-call | tf_op jit(solution)/shard_map/pallas_call | solution.py:536

commit v4 on v3

--- a/solution.py
+++ b/solution.py
@@ -236,16 +236,6 @@
     steps = [first_s, 6 - z - first_s - third_s, third_s]
     onward = [z + 1, z - 1, 3 * z - 3]
     middle = z * (3 - z) > 0
-    for sub in range(2):
-
-        @pl.when(z < nv - 1)
-        def _():
-            along(z, sub, zs.at[sub], z + 1).start()
-
-        @pl.when(z > 0)
-        def _():
-            along(z, sub, zs.at[2 + sub], z - 1).start()
-
     ccopies = [
         send(cpart, call.at[z], cs.at[k], cr.at[k], {"vocab": lax.rem(z + k, nv)})
         for k in range(1, nv)
@@ -254,6 +244,16 @@
     vcopies = [
         send(myval, vals.at[x, z], vs.at[k], vr.at[k], peers[k]) for k in range(nq - 1)
     ]
+
+    for sub in range(2):
+
+        @pl.when(z < nv - 1)
+        def _():
+            along(z, sub, zs.at[sub], z + 1).start()
+
+        @pl.when(z > 0)
+        def _():
+            along(z, sub, zs.at[2 + sub], z - 1).start()
 
     def pass_on(i):
         for sub in range(2):
@@ -288,6 +288,7 @@
     valid = to_row(valid_col, valid_col)
 
     pass_on(0)
+    pass_on(1)
     for d in ccopies:
         d.wait_recv()
     for d in vcopies:
@@ -310,7 +311,6 @@
         send(sqpart, sqall.at[z], qs.at[k], qr.at[k], {"vocab": lax.rem(z + k, nv)})
         for k in range(1, nv)
     ]
-    pass_on(1)
     pass_on(2)
     for d in qcopies:
         d.wait_recv()

time: 34.3 us -> 32.3 us (0.942)
  Pallas kernels: 33.5 us -> 31.4 us
    pallas_call x1, Pallas kernels: 32.2 us -> 30.1 us  [kernel_device(): pl.pallas_call(functools.partial(fused, nv), out_shape=shapes, in_specs=[...]
where the time goes in v4:
time: 32.3 us; the launch traced here: 32.1 us
  Pallas kernels  31.4 us (97%)
  between operations  0.64 us (2%)
    pallas_call x1, Pallas kernels, kernel_device(): pl.pallas_call(functools.partial(fused, nv), out_shape=shapes, in_specs=[...  30.1 us
    pallas_call x1, Pallas kernels, kernel_device(): pl.pallas_call(hand_out, out_shape=shapes, in_specs=[hbm] * 3, out_specs=...  1.29 us

profile of v4, /device:TPU:0, one launch (start us, length us, event | category | flops | bytes accessed | tf_op | source)
XLA Modules:
  0.0 32.1 jit_solution(2830975701204472180)
XLA Ops:
  0.6 30.1 %shard_map.112 = (f32[1,1024]{1,0:T(1,128)}, f32[1,64]{1,0:T(1,128)}, f32[1,64]{1,0:T(1,128)}) custom-call(s32[1,2]{1,0:T(1,128)} %bitcast.5, s32[1,64]{1,0:T(1,128)} %bitcast.6, s32[1,64]{1,0:T(1,128)} %bitcast.7, bf16[64,3584]{1,0:T(8,128)(2,1)} %act_hbm.1, bf16[4,3584]{1,0:T(4,128)(2,1)} %table_hbm.1, bf16[64,1024]{1,0:T(8,128)(2,1)} %base_hbm.1, ...), custom_call_target="tpu_custom_call" | custom-call | tf_op jit(solution)/shard_map/pallas_call | solution.py:485
  30.8 1.3 %shard_map.113 = (f32[1,1024]{1,0:T(1,128)}, f32[1,64]{1,0:T(1,128)}, f32[1,64]{1,0:T(1,128)}) custom-call(f32[1,1024]{1,0:T(1,128)} %get-tuple-element.6.a_ref, f32[1,64]{1,0:T(1,128)} %get-tuple-element.7.b_ref, f32[1,64]{1,0:T(1,128)} %get-tuple-element.8.c_ref), custom_call_target="tpu_custom_call" | custom-call | tf_op jit(solution)/shard_map/pallas_call | solution.py:536

commit v5 on v4

--- a/solution.py
+++ b/solution.py
@@ -241,19 +241,19 @@
         for k in range(1, nv)
     ]
 
+    for sub in range(2):
+
+        @pl.when(z < nv - 1)
+        def _():
+            along(z, sub, zs.at[sub], z + 1).start()
+
+        @pl.when(z > 0)
+        def _():
+            along(z, sub, zs.at[2 + sub], z - 1).start()
+
     vcopies = [
         send(myval, vals.at[x, z], vs.at[k], vr.at[k], peers[k]) for k in range(nq - 1)
     ]
-
-    for sub in range(2):
-
-        @pl.when(z < nv - 1)
-        def _():
-            along(z, sub, zs.at[sub], z + 1).start()
-
-        @pl.when(z > 0)
-        def _():
-            along(z, sub, zs.at[2 + sub], z - 1).start()
 
     def pass_on(i):
         for sub in range(2):

time: 32.3 us -> 32.1 us (level)
  no operation moved by 1% of the time
where the time goes in v5:
time: 32.1 us; the launch traced here: 31.9 us
  Pallas kernels  31.3 us (98%)
  between operations  0.64 us (2%)
    pallas_call x1, Pallas kernels, kernel_device(): pl.pallas_call(functools.partial(fused, nv), out_shape=shapes, in_specs=[...  30 us
    pallas_call x1, Pallas kernels, kernel_device(): pl.pallas_call(hand_out, out_shape=shapes, in_specs=[hbm] * 3, out_specs=...  1.29 us

profile of v5, /device:TPU:0, one launch (start us, length us, event | category | flops | bytes accessed | tf_op | source)
XLA Modules:
  0.0 31.9 jit_solution(10510381045816810789)
XLA Ops:
  0.6 30.0 %shard_map.112 = (f32[1,1024]{1,0:T(1,128)}, f32[1,64]{1,0:T(1,128)}, f32[1,64]{1,0:T(1,128)}) custom-call(s32[1,2]{1,0:T(1,128)} %bitcast.5, s32[1,64]{1,0:T(1,128)} %bitcast.6, s32[1,64]{1,0:T(1,128)} %bitcast.7, bf16[64,3584]{1,0:T(8,128)(2,1)} %act_hbm.1, bf16[4,3584]{1,0:T(4,128)(2,1)} %table_hbm.1, bf16[64,1024]{1,0:T(8,128)(2,1)} %base_hbm.1, ...), custom_call_target="tpu_custom_call" | custom-call | tf_op jit(solution)/shard_map/pallas_call | solution.py:485
  30.6 1.3 %shard_map.113 = (f32[1,1024]{1,0:T(1,128)}, f32[1,64]{1,0:T(1,128)}, f32[1,64]{1,0:T(1,128)}) custom-call(f32[1,1024]{1,0:T(1,128)} %get-tuple-element.6.a_ref, f32[1,64]{1,0:T(1,128)} %get-tuple-element.7.b_ref, f32[1,64]{1,0:T(1,128)} %get-tuple-element.8.c_ref), custom_call_target="tpu_custom_call" | custom-call | tf_op jit(solution)/shard_map/pallas_call | solution.py:536
